TPU v7x, 32 devices: a whole 2x2x4 slice. The times are simulated.
32 devices in a mesh: orient: 8 (over z, y), brow: 2 (over core), bcol: 2 (over x).
Axes of the slice: x: 2, y: 2, z: 4, core: 2. Of those that a mesh axis runs over, the one named last changes fastest.
Arguments:
- volume: float32 [8, 64, 208], P('orient', 'brow', 'bcol'), may hold values from -700 to 700
- template: float32 [24, 24, 24], replicated, may hold values from 0 to 1
- voxel_maps: int32 [8, 13824], P('orient'), may hold values from 0 to 13823, as said below
Outputs:
- best: float32 [8, 64, 208], P('orient', 'brow', 'bcol')
Inputs may be any that keep to these rules, and one draw needn't show every extreme that they name: `voxel_maps`: each row holds every number of 0 to 13823 exactly once.
All inputs are finite; a program needn't handle non-finite values.
Results may differ from a plain program's by a relative error of at most 0.00013.
Values sent between devices are 32-bit elements; how exact they have to be, the bound alone decides.
A program may use at most 64 MiB of HBM per device.

v0:
```python
import math

import jax
import jax.numpy as jnp
from jax import lax
from jax.sharding import PartitionSpec as P

epsilon = 1e-06
floor_share = 0.1
highest = lax.Precision.HIGHEST


def extended(cells, sides, width):
    for axis, dim in sides:
        count = lax.axis_size(axis)
        ends = count - 1
        head = lax.slice_in_dim(cells, 0, width, axis=dim)
        tail = lax.slice_in_dim(cells, cells.shape[dim] - width, cells.shape[dim], axis=dim)
        cells = jnp.concatenate(
            [
                lax.ppermute(tail, axis, [(i, (i + 1) % count) for i in range(ends)]),
                cells,
                lax.ppermute(head, axis, [((i + 1) % count, i) for i in range(ends)]),
            ],
            axis=dim,
        )
    return cells


def phase_tables(row_index, col_index, length):
    products = row_index[:, None] * col_index[None, :] % length
    angles = products.astype(jnp.float32) * (2.0 * math.pi / length)
    return (jnp.cos(angles), jnp.sin(angles))


def band_table(row_index, col_index, lower, upper):
    offsets = col_index[None, :] - row_index[:, None]
    return ((offsets >= lower) & (offsets < upper)).astype(jnp.float32)


def whiten_rows(rows_in):
    length = rows_in.shape[-1]
    frequency = jnp.arange(length, dtype=jnp.int32)
    cosine, sine_table = phase_tables(frequency, frequency, length)
    spec_real = jnp.dot(rows_in, cosine, precision=highest)
    spec_imag = -jnp.dot(rows_in, sine_table, precision=highest)
    power_spec = spec_real * spec_real + spec_imag * spec_imag
    smoothed = (
        jnp.roll(power_spec, 1, axis=1) + power_spec + jnp.roll(power_spec, -1, axis=1)
    ) / 3.0
    smoothed = smoothed + floor_share * jnp.mean(power_spec, axis=1, keepdims=True) + epsilon
    weights = lax.rsqrt(smoothed)
    whitened = jnp.dot(spec_real * weights, cosine, precision=highest) - jnp.dot(
        spec_imag * weights, sine_table, precision=highest
    )
    return whitened / math.sqrt(length)


def shards(volume, template, voxel_maps):
    plane_count, brick_rows, brick_cols = volume.shape
    template_edge = template.shape[0]
    half_edge = template_edge // 2
    depth_total = plane_count * lax.axis_size("orient")
    pad_rows = brick_rows + template_edge
    pad_cols = brick_cols + template_edge
    pad_depth = depth_total + template_edge
    pencils = lax.all_to_all(volume, "bcol", split_axis=1, concat_axis=2, tiled=True)
    whitened_rows = whiten_rows(pencils.reshape(-1, pencils.shape[-1])).reshape(pencils.shape)
    whitened = lax.all_to_all(whitened_rows, "bcol", split_axis=2, concat_axis=1, tiled=True)
    padded = extended(whitened, (("brow", 1), ("bcol", 2)), half_edge)
    col_freq = jnp.arange(pad_cols, dtype=jnp.int32)
    row_freq = jnp.arange(pad_rows, dtype=jnp.int32)
    depth_freq = jnp.arange(pad_depth, dtype=jnp.int32)
    depth_index = jnp.arange(depth_total, dtype=jnp.int32)
    tpl_index = jnp.arange(template_edge, dtype=jnp.int32)
    out_rows = jnp.arange(brick_rows, dtype=jnp.int32)
    out_cols = jnp.arange(brick_cols, dtype=jnp.int32)
    cos_cols, sin_cols = phase_tables(col_freq, col_freq, pad_cols)
    cos_rows, sin_rows = phase_tables(row_freq, row_freq, pad_rows)
    cos_depth, sin_depth = phase_tables(depth_freq, depth_index, pad_depth)
    tcos_cols, tsin_cols = phase_tables(tpl_index, col_freq, pad_cols)
    tcos_rows, tsin_rows = phase_tables(row_freq, tpl_index, pad_rows)
    tcos_depth, tsin_depth = phase_tables(depth_freq, tpl_index, pad_depth)
    back_depth_c, back_depth_s = phase_tables(depth_index - half_edge, depth_freq, pad_depth)
    back_rows_c, back_rows_s = phase_tables(out_rows, row_freq, pad_rows)
    back_cols_c, back_cols_s = phase_tables(col_freq, out_cols, pad_cols)
    box_rows = band_table(out_rows, row_freq, 0, template_edge)
    box_cols = band_table(out_cols, col_freq, 0, template_edge).T
    box_depth = band_table(depth_index, depth_index, -half_edge, half_edge)
    portion = lax.all_gather(padded, "orient", axis=0, tiled=True)
    col_real = jnp.einsum("nxy,yk->nxk", portion, cos_cols, precision=highest)
    col_imag = -jnp.einsum("nxy,yk->nxk", portion, sin_cols, precision=highest)
    spec_real = jnp.einsum("kx,nxy->nky", cos_rows, col_real, precision=highest) + jnp.einsum(
        "kx,nxy->nky", sin_rows, col_imag, precision=highest
    )
    spec_imag = jnp.einsum("kx,nxy->nky", cos_rows, col_imag, precision=highest) - jnp.einsum(
        "kx,nxy->nky", sin_rows, col_real, precision=highest
    )
    squares = portion * portion
    along_cols = jnp.einsum("nxy,yr->nxr", squares, box_cols, precision=highest)
    sum_real = jnp.einsum("kz,zxy->kxy", cos_depth, spec_real, precision=highest) + jnp.einsum(
        "kz,zxy->kxy", sin_depth, spec_imag, precision=highest
    )
    sum_imag = jnp.einsum("kz,zxy->kxy", cos_depth, spec_imag, precision=highest) - jnp.einsum(
        "kz,zxy->kxy", sin_depth, spec_real, precision=highest
    )
    sum_energy = jnp.einsum(
        "wz,zqr->wqr",
        box_depth,
        jnp.einsum("qx,nxr->nqr", box_rows, along_cols, precision=highest),
        precision=highest,
    )
    flattened = template.reshape(-1)
    centred = flattened - jnp.mean(flattened)
    normed = centred / jnp.sqrt(jnp.sum(centred * centred) + epsilon)
    voxel_total = flattened.shape[0]
    scaling = lax.rsqrt(sum_energy / voxel_total + epsilon)
    inverse_norm = 1.0 / (pad_depth * pad_rows * pad_cols)
    rotated = normed[voxel_maps[0]].reshape(template_edge, template_edge, template_edge)
    tcol_real = jnp.einsum("abc,ck->abk", rotated, tcos_cols, precision=highest)
    tcol_imag = -jnp.einsum("abc,ck->abk", rotated, tsin_cols, precision=highest)
    trow_real = jnp.einsum("kb,abc->akc", tcos_rows, tcol_real, precision=highest) + jnp.einsum(
        "kb,abc->akc", tsin_rows, tcol_imag, precision=highest
    )
    trow_imag = jnp.einsum("kb,abc->akc", tcos_rows, tcol_imag, precision=highest) - jnp.einsum(
        "kb,abc->akc", tsin_rows, tcol_real, precision=highest
    )
    tpl_real = jnp.einsum("ka,abc->kbc", tcos_depth, trow_real, precision=highest) + jnp.einsum(
        "ka,abc->kbc", tsin_depth, trow_imag, precision=highest
    )
    tpl_imag = jnp.einsum("ka,abc->kbc", tcos_depth, trow_imag, precision=highest) - jnp.einsum(
        "ka,abc->kbc", tsin_depth, trow_real, precision=highest
    )
    prod_real = sum_real * tpl_real + sum_imag * tpl_imag
    prod_imag = sum_imag * tpl_real - sum_real * tpl_imag
    depth_real = jnp.einsum("zk,kxy->zxy", back_depth_c, prod_real, precision=highest) - jnp.einsum(
        "zk,kxy->zxy", back_depth_s, prod_imag, precision=highest
    )
    depth_imag = jnp.einsum("zk,kxy->zxy", back_depth_c, prod_imag, precision=highest) + jnp.einsum(
        "zk,kxy->zxy", back_depth_s, prod_real, precision=highest
    )
    rows_real = jnp.einsum("qk,zky->zqy", back_rows_c, depth_real, precision=highest) - jnp.einsum(
        "qk,zky->zqy", back_rows_s, depth_imag, precision=highest
    )
    rows_imag = jnp.einsum("qk,zky->zqy", back_rows_c, depth_imag, precision=highest) + jnp.einsum(
        "qk,zky->zqy", back_rows_s, depth_real, precision=highest
    )
    correlation = jnp.einsum("zqk,kr->zqr", rows_real, back_cols_c, precision=highest) - jnp.einsum(
        "zqk,kr->zqr", rows_imag, back_cols_s, precision=highest
    )
    score = correlation * inverse_norm * scaling
    received = lax.all_to_all(score[None], "orient", split_axis=1, concat_axis=0, tiled=True)
    return jnp.max(received, axis=0)


def solution(mesh):
    in_specs = (P("orient", "brow", "bcol"), P(), P("orient", None))
    out_specs = P("orient", "brow", "bcol")
    return jax.shard_map(shards, mesh=mesh, in_specs=in_specs, out_specs=out_specs, check_vma=False)
```

profile of v0, /device:TPU:0, one launch (start us, length us, event | category | flops | bytes accessed | tf_op | source)
XLA Modules:
  0.0 171.4 jit_solution(4194441242745127263)
XLA Ops:
  0.0 4.4 %all-to-all-start = ((f32[1,32,104]{2,0,1:T(1,128)}), f32[1,32,104]{2,0,1:T(1,128)S(1)}, u32[]{:S(2)}, u32[]{:S(2)}) async-start(f32[1,32,104]{2,0,1:T(1,128)} %bitcast.159), calls=%async_computation | async-start | bytes 32768 | tf_op jit(solution)/shard_map/all_to_all | solution.py:67
  4.4 1.6 reduce_sum.28
  6.7 0.7 multiply_reduce_fusion
  8.5 71.2 %gather_fusion = f32[13824]{0:T(1024)S(1)} fusion(f32[13824]{0:T(1024)S(1)} %div.38, s32[14336]{0:T(1024)S(1)} %pad_clamp_fusion), kind=kCustom, calls=%fused_computation | custom fusion | bytes 165888 | tf_op jit(solution)/shard_map/gather | solution.py:119
  79.9 0.4 convolution_negate_fusion
  80.8 0.8 fusion.167
  81.6 0.8 fusion.165
  82.4 0.8 fusion.1
  83.2 0.8 fusion
  84.1 1.0 fusion.11
  85.1 1.0 convolution_subtract_fusion
  86.2 1.0 convolution_bitcast_fusion.1
  87.2 1.2 fusion.392
  88.6 1.0 fusion.37
  89.6 1.1 fusion.10
  90.8 0.6 broadcast.170
  91.4 0.9 reduce.7
  92.3 0.7 reshape.87
  93.0 3.4 %all-to-all-start.1 = ((f32[2,1,1664]{2,1,0:T(1,128)}), f32[2,1,1664]{2,1,0:T(1,128)S(1)}, u32[]{:S(2)}, u32[]{:S(2)}) async-start(f32[2,1,1664]{2,1,0:T(1,128)} %reshape.87), calls=%async_computation.1 | async-start | bytes 26624 | tf_op jit(solution)/shard_map/all_to_all | solution.py:69
  96.5 1.0 fusion.15
  97.4 2.8 %all-to-all-done.1 = f32[2,1,1664]{2,1,0:T(1,128)S(1)} async-done(((f32[2,1,1664]{2,1,0:T(1,128)}), f32[2,1,1664]{2,1,0:T(1,128)S(1)}, u32[]{:S(2)}, u32[]{:S(2)}) %all-to-all-start.1) | async-done | bytes 13344 | tf_op jit(solution)/shard_map/all_to_all | solution.py:69
  100.3 0.7 reduce.8
  101.3 1.3 collective-permute-start
  102.6 1.3 collective-permute-start.1
  103.9 1.0 convolution_add_fusion
  104.9 0.8 collective-permute-done.1
  105.8 1.9 %collective-permute-start.2 = (f32[1,56,12]{2,1,0:T(8,128)S(1)}, f32[1,56,12]{2,1,0:T(8,128)S(1)}, u32[]{:S(2)}, u32[]{:S(2)}) collective-permute-start(f32[1,56,12]{2,1,0:T(8,128)S(1)} %get-tuple-element.9), channel_id=1, source_target_pairs={{0,1},{2,3},{4,5},{6,7},{8,9},{10,11},{12,13},{14,15},{16,17},{18,... | collective-permute-start | bytes 8072 | tf_op jit(solution)/shard_map/ppermute | solution.py:21
  107.7 1.3 collective-permute-start.3
  109.2 4.2 %collective-permute-done.3 = f32[1,56,12]{2,1,0:T(8,128)S(1)} collective-permute-done((f32[1,56,12]{2,1,0:T(8,128)S(1)}, f32[1,56,12]{2,1,0:T(8,128)S(1)}, u32[]{:S(2)}, u32[]{:S(2)}) %collective-permute-start.3) | collective-permute-done | bytes 2720 | tf_op jit(solution)/shard_map/ppermute | solution.py:23
  113.5 31.5 %all_gather.3 = f32[8,56,128]{2,1,0:T(8,128)S(1)} all-gather(f32[1,56,128]{2,1,0:T(8,128)S(1)} %pad_maximum_fusion.1), channel_id=1, replica_groups=mesh['orient'=8,'brow'=2,'bcol'=2] {'orient'}, dimensions={0}, use_global_device_ids=true | all-gather | bytes 258048 | tf_op jit(solution)/shard_map/all_gather | solution.py:90
  145.0 0.6 convolution_negate_fusion.1
  145.6 0.6 fusion.64
  147.0 0.5 fusion.97
  147.5 0.5 fusion.95
  148.0 0.5 fusion.3
  148.5 0.5 fusion.2
  149.0 1.0 fusion.25
  149.9 1.0 fusion.29
  150.9 1.0 convolution_subtract_fusion.1
  151.9 1.2 multiply_subtract_fusion
  153.1 0.6 fusion.236
  153.7 0.6 fusion.238
  154.3 0.6 convolution_add_fusion.4
  155.0 0.6 convolution_subtract_fusion.4
  157.2 0.5 fusion.76
  157.6 0.5 fusion.6
  158.1 12.7 %all_to_all.42 = f32[1,8,32,104]{3,2,0,1:T(8,128)S(1)} all-to-all(f32[1,8,32,104]{3,2,0,1:T(8,128)S(1)} %fusion.6), channel_id=1, replica_groups=mesh['orient'=8,'brow'=2,'bcol'=2] {'orient'}, dimensions={1} | all-to-all | bytes 212992 | tf_op jit(solution)/shard_map/all_to_all | solution.py:152
  170.8 0.6 reduce_max.11
  (34 shorter events, 4.5 us)
Async XLA Ops:
  0.0 6.7 %copy-start = (f32[24,24,24]{2,1,0:T(8,128)S(1)}, f32[24,24,24]{2,1,0:T(8,128)}, u32[]{:S(2)}) copy-start(f32[24,24,24]{2,1,0:T(8,128)} %param.4) | copy-start | bytes 165892
  0.0 86.0 %all-to-all-start = ((f32[1,32,104]{2,0,1:T(1,128)}), f32[1,32,104]{2,0,1:T(1,128)S(1)}, u32[]{:S(2)}, u32[]{:S(2)}) async-start(f32[1,32,104]{2,0,1:T(1,128)} %bitcast.159), calls=%async_computation | async-start | bytes 32768 | tf_op jit(solution)/shard_map/all_to_all | solution.py:67
  6.7 1.4 copy-start.1
  93.0 7.2 %all-to-all-start.1 = ((f32[2,1,1664]{2,1,0:T(1,128)}), f32[2,1,1664]{2,1,0:T(1,128)S(1)}, u32[]{:S(2)}, u32[]{:S(2)}) async-start(f32[2,1,1664]{2,1,0:T(1,128)} %reshape.87), calls=%async_computation.1 | async-start | bytes 26624 | tf_op jit(solution)/shard_map/all_to_all | solution.py:69
  101.3 3.6 %collective-permute-start = (f32[1,12,104]{2,1,0:T(8,128)S(1)}, f32[1,12,104]{2,1,0:T(8,128)S(1)}, u32[]{:S(2)}, u32[]{:S(2)}) collective-permute-start(f32[1,12,104]{2,1,0:T(8,128)S(1)} %get-tuple-element.11), channel_id=1, source_target_pairs={{0,2},{1,3},{4,6},{5,7},{8,10},{9,11},{12,14},{13,15},{16,18},{17,... | collective-permute-start | bytes 14984 | tf_op jit(solution)/shard_map/ppermute | solution.py:21
  102.6 3.1 %collective-permute-start.1 = (f32[1,12,104]{2,1,0:T(8,128)S(1)}, f32[1,12,104]{2,1,0:T(8,128)S(1)}, u32[]{:S(2)}, u32[]{:S(2)}) collective-permute-start(f32[1,12,104]{2,1,0:T(8,128)S(1)} %get-tuple-element.12), channel_id=1, source_target_pairs={{2,0},{3,1},{6,4},{7,5},{10,8},{11,9},{14,12},{15,13},{18,16},{19,... | collective-permute-start | bytes 14984 | tf_op jit(solution)/shard_map/ppermute | solution.py:23
  105.8 3.5 %collective-permute-start.2 = (f32[1,56,12]{2,1,0:T(8,128)S(1)}, f32[1,56,12]{2,1,0:T(8,128)S(1)}, u32[]{:S(2)}, u32[]{:S(2)}) collective-permute-start(f32[1,56,12]{2,1,0:T(8,128)S(1)} %get-tuple-element.9), channel_id=1, source_target_pairs={{0,1},{2,3},{4,5},{6,7},{8,9},{10,11},{12,13},{14,15},{16,17},{18,... | collective-permute-start | bytes 8072 | tf_op jit(solution)/shard_map/ppermute | solution.py:21
  107.7 5.8 %collective-permute-start.3 = (f32[1,56,12]{2,1,0:T(8,128)S(1)}, f32[1,56,12]{2,1,0:T(8,128)S(1)}, u32[]{:S(2)}, u32[]{:S(2)}) collective-permute-start(f32[1,56,12]{2,1,0:T(8,128)S(1)} %get-tuple-element.10), channel_id=1, source_target_pairs={{1,0},{3,2},{5,4},{7,6},{9,8},{11,10},{13,12},{15,14},{17,16},{19,... | collective-permute-start | bytes 8072 | tf_op jit(solution)/shard_map/ppermute | solution.py:23
where the time goes:
time: 172 us; the launch traced here: 171 us
  local copies, waits for them, and re-layouts  73.6 us (43%)
  blocking collectives  44.2 us (26%)
  matrix products  25.2 us (15%)
  starting transfers between devices  13.6 us (8%)
  waiting for transfers between devices  8.06 us (5%)
  other arithmetic  5.04 us (3%)
  between operations  1.8 us (1%)
    gather x1, local copies, waits for them, and re-layouts, shards(): normed[voxel_maps[0]].reshape(template_edge, template_edge, template_edge)  71.2 us
    all_gather x1, blocking collectives, shards(): portion = lax.all_gather(padded, 'orient', axis=0, tiled=True)  31.5 us
    all_to_all x1, blocking collectives, shards(): lax.all_to_all(score[None], 'orient', split_axis=1, concat_axis=0, tiled=...  12.7 us
    ppermute x2, waiting for transfers between devices, extended(): lax.ppermute(head, axis, [((i + 1) % count, i) for i in range(ends)])  4.99 us
    all_to_all x1, starting transfers between devices, shards(): lax.all_to_all(volume, 'bcol', split_axis=1, concat_axis=2, tiled=True)  4.37 us
  transfers between devices with their start and end apart: 6, of which 4 were waited for; matrix products, arithmetic and copies ran while one was open for 48% of the time, Pallas kernels for 0%

commit v1 on v0

v1 whole, which is shorter than its diff:
```python
import math

import numpy as np
import jax
import jax.numpy as jnp
from jax import lax
from jax.experimental import pallas as pl
from jax.experimental.pallas import tpu as pltpu
from jax.sharding import PartitionSpec as P

epsilon = 1e-06
floor_share = 0.1
highest = lax.Precision.HIGHEST
LANES = 128
MESH = pl.DeviceIdType.MESH


def round_up(value, step):
    return -(-value // step) * step


def forward_table(length, parts):
    half = length // 2 + 1
    padded = round_up(half, LANES)
    angles = 2.0 * np.pi * (np.outer(np.arange(length), np.arange(half)) % length) / length
    table = np.zeros((length, 2 * padded))
    table[:, :half] = np.cos(angles)
    table[:, padded : padded + half] = -np.sin(angles)
    return table.reshape(parts, length // parts, 2 * padded).astype(np.float32)


def smoothing_table(length):
    half = length // 2 + 1
    padded = round_up(half, LANES)
    table = np.zeros((padded, padded))
    fold = np.minimum(np.arange(length), length - np.arange(length))
    for k in range(half):
        for shift in (-1, 0, 1):
            table[fold[(k + shift) % length], k] += 1.0 / 3.0
        for other in range(length):
            table[fold[other], k] += floor_share / length
    return table.astype(np.float32)


def windowed_inverse(length, parts, margin):
    half = length // 2 + 1
    padded = round_up(half, LANES)
    width = length // parts
    tables = np.zeros((parts, 2 * padded, width + 2 * margin))
    k = np.arange(half)
    share = np.where((k == 0) | (2 * k == length), 1.0, 2.0)[:, None] / math.sqrt(length)
    for part in range(parts):
        columns = np.arange(width + 2 * margin) + part * width - margin
        inside = (columns >= 0) & (columns < length)
        angles = 2.0 * np.pi * (np.outer(k, columns) % length) / length
        tables[part, :half] = share * np.cos(angles) * inside
        tables[part, padded : padded + half] = -share * np.sin(angles) * inside
    return tables.astype(np.float32)


def packed_dft(count, size):
    k = np.arange(size)
    real = k <= size // 2
    freq = np.where(real, k, k - size // 2)
    angles = 2.0 * np.pi * (np.outer(np.arange(count), freq) % size) / size
    return angles, real, freq


def volume_table(size):
    angles, real, freq = packed_dft(size, size)
    return np.where(real, np.cos(angles), -np.sin(angles)).astype(np.float32)


def template_table(count, size):
    angles, real, freq = packed_dft(count, size)
    straight = np.cos(angles)
    edge = (freq == 0) | (freq == size // 2)
    crossed = np.where(real, -np.sin(angles), np.sin(angles)) * ~edge
    return np.concatenate([straight, crossed], axis=1).astype(np.float32)


def score_table(size, count):
    angles, real, freq = packed_dft(count, size)
    share = np.where((freq == 0) | (freq == size // 2), 1.0, 2.0)
    return (np.where(real, np.cos(angles), -np.sin(angles)) * share / size).T.astype(np.float32)


def box_table(size, count, edge):
    offsets = np.arange(size)[:, None] - np.arange(count)[None, :]
    return ((offsets >= 0) & (offsets < edge)).astype(np.float32)


def dot(a, b):
    return jnp.dot(a, b, precision=highest, preferred_element_type=jnp.float32)


def rotate_kernel(voxels, lead, table_ref, index_ref, dft_ref, straight_ref, crossed_ref, normed, rotated):
    table = table_ref[...]
    rows = table.shape[0]
    flat = lax.broadcasted_iota(jnp.int32, table.shape, 0) * LANES + lax.broadcasted_iota(
        jnp.int32, table.shape, 1
    )
    valid = flat < voxels
    mean = jnp.sum(table, keepdims=True) / voxels
    centred = jnp.where(valid, table - mean, 0.0)
    normed[...] = centred / jnp.sqrt(jnp.sum(centred * centred, keepdims=True) + epsilon)
    edge, width = index_ref.shape
    tiles = [(s, c) for s in range(0, edge, 8) for c in range(0, width, LANES)]
    lows, highs = [], []
    for s, c in tiles:
        index = index_ref[s : s + 8, c : c + LANES]
        lows.append(index & (LANES - 1))
        highs.append(index >> 7)

    def step(h, held):
        row = jnp.broadcast_to(normed[pl.ds(h, 1), :], (8, LANES))
        return tuple(
            jnp.where(high == h, jnp.take_along_axis(row, low, axis=1), value)
            for low, high, value in zip(lows, highs, held)
        )

    zero = jnp.zeros((8, LANES), jnp.float32)
    held = lax.fori_loop(0, rows, step, tuple(zero for _ in tiles))
    for (s, c), value in zip(tiles, held):
        rotated[s : s + 8, c : c + LANES] = value
    spectrum = lax.dot_general(
        rotated[...],
        dft_ref[...],
        (((0,), (0,)), ((), ())),
        precision=highest,
        preferred_element_type=jnp.float32,
    )
    size = spectrum.shape[1] // 2
    if straight_ref.shape[0] > edge:
        straight_ref[...] = jnp.zeros_like(straight_ref)
        crossed_ref[...] = jnp.zeros_like(crossed_ref)
    straight_ref[lead : lead + edge] = spectrum[: edge * edge, :size].reshape(edge, edge, size)
    crossed_ref[lead : lead + edge] = spectrum[: edge * edge, size:].reshape(edge, edge, size)


def match_kernel(
    sizes,
    brick_ref,
    straight_ref,
    crossed_ref,
    forward_ref,
    smoothing_ref,
    inverse_ref,
    volume_dft_ref,
    score_dft_ref,
    box_ref,
    best_ref,
    pencils,
    tall,
    windows,
    spectrum,
    swapped,
    energy,
    totals,
    scores,
    arrived,
    sems1,
    sems2,
    sems3,
):
    orients, brows, bcols, edge, voxels, lead = sizes
    half_edge = edge // 2
    rows, cols = brick_ref.shape[1:]
    tile_rows = windows.shape[1]
    me = lax.axis_index("orient")
    row_id = lax.axis_index("brow")
    col_id = lax.axis_index("bcol")
    group = brows * bcols
    place = row_id * bcols + col_id

    def brick_peer(step):
        other = lax.rem(place + step, group)
        return {"orient": me, "brow": other // bcols, "bcol": lax.rem(other, bcols)}

    def plane_peer(step):
        return {"orient": lax.rem(me + step, orients), "brow": row_id, "bcol": col_id}

    barrier = pltpu.get_barrier_semaphore()
    for step in range(1, group):
        pl.semaphore_signal(barrier, inc=1, device_id=brick_peer(step), device_id_type=MESH)
    for step in range(1, orients):
        pl.semaphore_signal(barrier, inc=1, device_id=plane_peer(step), device_id_type=MESH)
    pl.semaphore_wait(barrier, group + orients - 2)

    gathers = []
    for step in range(1, group):
        copy = pltpu.make_async_remote_copy(
            src_ref=brick_ref.at[0],
            dst_ref=pencils.at[col_id, row_id],
            send_sem=sems1.at[0, step],
            recv_sem=sems1.at[1, step],
            device_id=brick_peer(step),
            device_id_type=MESH,
        )
        copy.start()
        gathers.append(copy)
    pencils[col_id, row_id] = brick_ref[0]
    energy[...] = jnp.zeros_like(energy)
    totals[...] = jnp.zeros_like(totals)
    tall[...] = jnp.zeros_like(tall)
    for copy in gathers:
        copy.wait_recv()

    both = None
    for part in range(bcols):
        term = dot(pencils[part].reshape(brows * rows, cols), forward_ref[part])
        both = term if both is None else both + term
    padded = both.shape[1] // 2
    real, imag = both[:, :padded], both[:, padded:]
    weights = lax.rsqrt(dot(real * real + imag * imag, smoothing_ref[...]) + epsilon)
    tall[half_edge : half_edge + brows * rows, :] = dot(
        real * weights, inverse_ref[col_id, :padded, :]
    ) + dot(imag * weights, inverse_ref[col_id, padded:, :])
    start = pl.multiple_of(row_id * rows, 8)
    windows[me] = tall[pl.ds(start, tile_rows), :]

    sends = []
    for step in range(1, orients):
        copy = pltpu.make_async_remote_copy(
            src_ref=windows.at[me],
            dst_ref=windows.at[me],
            send_sem=sems2.at[0, step],
            recv_sem=sems2.at[1, step],
            device_id=plane_peer(step),
            device_id_type=MESH,
        )
        copy.start()
        sends.append(copy)

    bunch = math.gcd(orients, 8)

    def absorb(plane):
        window = windows[plane]
        gap = plane - me
        near = jnp.logical_and(gap >= -half_edge, gap < half_edge).astype(jnp.float32)
        energy[...] += window * window * near
        transformed = dot(window, volume_dft_ref[...])
        spectrum[...] = transformed
        swapped[...] = pltpu.roll(transformed, transformed.shape[1] // 2, 1)

        def targets(piece):
            first = piece * bunch
            held = [totals[first + z] for z in range(bunch)]
            for b in range(edge):
                near_part = spectrum[b : b + rows, :]
                far_part = swapped[b : b + rows, :]
                for z in range(bunch):
                    a = plane - first - z + half_edge + lead
                    held[z] = held[z] + (
                        near_part * straight_ref[a, b : b + 1, :]
                        + far_part * crossed_ref[a, b : b + 1, :]
                    )
            for z in range(bunch):
                totals[first + z] = held[z]

        if orients == bunch:
            targets(0)
        else:
            pl.loop(0, orients // bunch)(targets)

    absorb(me)

    @pl.loop(1, orients)
    def _(step):
        source = lax.rem(me - step + orients, orients)
        pltpu.make_async_remote_copy(
            src_ref=windows.at[source],
            dst_ref=windows.at[source],
            send_sem=sems2.at[0, step],
            recv_sem=sems2.at[1, step],
            device_id=plane_peer(step),
            device_id_type=MESH,
        ).wait_recv()
        absorb(source)

    size = spectrum.shape[1]
    scored = dot(totals[...].reshape(orients * rows, size), score_dft_ref[...])
    scores[...] = scored.reshape(orients, rows, cols)
    returns = []
    for step in range(1, orients):
        copy = pltpu.make_async_remote_copy(
            src_ref=scores.at[lax.rem(me + step, orients)],
            dst_ref=arrived.at[step],
            send_sem=sems3.at[0, step],
            recv_sem=sems3.at[1, step],
            device_id=plane_peer(step),
            device_id_type=MESH,
        )
        copy.start()
        returns.append(copy)
    summed = energy[0:rows, :]
    for b in range(1, edge):
        summed = summed + energy[b : b + rows, :]
    scaling = lax.rsqrt(dot(summed, box_ref[...]) / voxels + epsilon)
    best = scores[me]
    for step, copy in zip(range(1, orients), returns):
        copy.wait_recv()
        best = jnp.maximum(best, arrived[step])
    best_ref[0] = best * scaling
    for copy in gathers + sends + returns:
        copy.wait_send()


def shards(volume, template, voxel_maps):
    orients, brows, bcols = (lax.axis_size(axis) for axis in ("orient", "brow", "bcol"))
    planes, rows, cols = volume.shape
    edge = template.shape[0]
    half_edge = edge // 2
    voxels = edge**3
    length = cols * bcols
    size = cols + edge
    tile_rows = rows + edge
    table_rows = round_up(voxels, LANES) // LANES
    table = jnp.pad(template.reshape(-1), (0, table_rows * LANES - voxels)).reshape(table_rows, LANES)
    width = round_up(edge * edge, LANES)
    index = jnp.pad(voxel_maps[0].reshape(edge * edge, edge).T, ((0, 0), (0, width - edge * edge)))
    lead = max(0, orients - 1 - half_edge)
    trail = max(0, half_edge + orients - edge)
    vmem = pl.BlockSpec(memory_space=pltpu.VMEM)
    spectra = jax.ShapeDtypeStruct((lead + edge + trail, edge, size), jnp.float32)
    straight, crossed = pl.pallas_call(
        lambda *refs: rotate_kernel(voxels, lead, *refs),
        out_shape=(spectra, spectra),
        in_specs=[vmem] * 3,
        out_specs=(vmem, vmem),
        scratch_shapes=[
            pltpu.VMEM((table_rows, LANES), jnp.float32),
            pltpu.VMEM((edge, width), jnp.float32),
        ],
        name="rotate",
    )(table, index, jnp.asarray(template_table(edge, size)))
    constants = (
        forward_table(length, bcols),
        smoothing_table(length),
        windowed_inverse(length, bcols, half_edge),
        volume_table(size),
        score_table(size, cols),
        box_table(size, cols, edge),
    )
    sizes = (orients, brows, bcols, edge, voxels, lead)
    return pl.pallas_call(
        lambda *refs: match_kernel(sizes, *refs),
        out_shape=jax.ShapeDtypeStruct((1, rows, cols), jnp.float32),
        in_specs=[vmem] * 9,
        out_specs=vmem,
        scratch_shapes=[
            pltpu.VMEM((bcols, brows, rows, cols), jnp.float32),
            pltpu.VMEM((brows * rows + edge, size), jnp.float32),
            pltpu.VMEM((orients, tile_rows, size), jnp.float32),
            pltpu.VMEM((tile_rows, size), jnp.float32),
            pltpu.VMEM((tile_rows, size), jnp.float32),
            pltpu.VMEM((tile_rows, size), jnp.float32),
            pltpu.VMEM((orients, rows, size), jnp.float32),
            pltpu.VMEM((orients, rows, cols), jnp.float32),
            pltpu.VMEM((orients, rows, cols), jnp.float32),
            pltpu.SemaphoreType.DMA((2, brows * bcols)),
            pltpu.SemaphoreType.DMA((2, orients)),
            pltpu.SemaphoreType.DMA((2, orients)),
        ],
        compiler_params=pltpu.CompilerParams(collective_id=0, has_side_effects=True),
        name="match",
    )(volume, straight, crossed, *(jnp.asarray(c) for c in constants))


def solution(mesh):
    in_specs = (P("orient", "brow", "bcol"), P(), P("orient", None))
    out_specs = P("orient", "brow", "bcol")
    return jax.shard_map(shards, mesh=mesh, in_specs=in_specs, out_specs=out_specs, check_vma=False)
```

time: 172 us -> 44.8 us (0.26)
  local copies, waits for them, and re-layouts: 73.6 us -> 4.05 us
  blocking collectives: 44.2 us -> 0 us
  Pallas kernels: 0 us -> 40.3 us
  matrix products: 25.2 us -> 0 us
  starting transfers between devices: 13.6 us -> 0 us
  waiting for transfers between devices: 8.06 us -> 0 us
  other arithmetic: 5.04 us -> 0.13 us
  between operations: 1.8 us -> 0.02 us
    gather x1 -> x0, local copies, waits for them, and re-layouts: 71.2 us -> none  [shards(): normed[voxel_maps[0]].reshape(template_edge, template_edge, template_edge)]
    pallas_call x0 -> x2, Pallas kernels: none -> 40.3 us  [the longest x1 26.2 us: shards(): pl.pallas_call(lambda *refs: match_kernel(sizes, *refs), out_shape=jax.Sh...]
    all_gather x1 -> x0, blocking collectives: 31.5 us -> none  [shards(): portion = lax.all_gather(padded, 'orient', axis=0, tiled=True)]
    dot_general x37 -> x0, matrix products: 25.2 us -> none  [the longest x1 1.21 us: shards(): jnp.einsum('kz,zxy->kxy', sin_depth, spec_imag, precision=highest)]
    all_to_all x1 -> x0, blocking collectives: 12.7 us -> none  [shards(): lax.all_to_all(score[None], 'orient', split_axis=1, concat_axis=0, tiled=...]
    all_to_all x2 -> x0, starting transfers between devices: 7.78 us -> none  [the longest x1 4.37 us: shards(): lax.all_to_all(volume, 'bcol', split_axis=1, concat_axis=2, tiled=True)]
    ppermute x4 -> x0, starting transfers between devices: 5.79 us -> none  [the longest x2 3.2 us: extended(): lax.ppermute(tail, axis, [(i, (i + 1) % count) for i in range(ends)])]
    ppermute x4 -> x0, waiting for transfers between devices: 5.22 us -> none  [the longest x2 4.99 us: extended(): lax.ppermute(head, axis, [((i + 1) % count, i) for i in range(ends)])]
  transfers between devices with their start and end apart: 6 -> 0, of which waited for: 4 -> 0; matrix products, arithmetic and copies ran while one was open for 48% -> 0% of each run, Pallas kernels for 0% -> 0%
where the time goes in v1:
time: 44.8 us; the launch traced here: 44.5 us
  Pallas kernels  40.3 us (90%)
  local copies, waits for them, and re-layouts  4.05 us (9%)
    pallas_call x1, Pallas kernels, shards(): pl.pallas_call(lambda *refs: match_kernel(sizes, *refs), out_shape=jax.Sh...  26.2 us
    pallas_call x1, Pallas kernels, shards(): pl.pallas_call(lambda *refs: rotate_kernel(voxels, lead, *refs), out_shap...  14.1 us
    reshape x1, local copies, waits for them, and re-layouts, shards(): jnp.pad(template.reshape(-1), (0, table_rows * LANES - voxels))  1.76 us
    unnamed x3, local copies, waits for them, and re-layouts  1.33 us

profile of v1, /device:TPU:0, one launch (start us, length us, event | category | flops | bytes accessed | tf_op | source)
XLA Modules:
  0.0 44.5 jit_solution(14347820791228096339)
XLA Ops:
  0.0 0.0 copy-start
  0.0 1.8 %reshape.5.refs_0_ = f32[108,128]{1,0:T(8,128)} reshape(f32[24,24,24]{2,1,0:T(8,128)} %param.11) | data formatting | bytes 110592 | tf_op jit(solution)/shard_map/reshape | solution.py:319
  1.8 0.0 copy-done
  1.8 0.1 reduce
  1.9 0.2 reshape_squeeze.3
  2.1 0.1 copy.11
  2.2 0.6 %pad.4.refs_1_ = s32[24,640]{1,0:T(8,128)} pad(s32[24,576]{1,0:T(8,128)S(1)} %bitcast.1, s32[]{:T(128)} %constant.7.clone.1), padding=0_0x0_64 | pad | bytes 116740 | tf_op jit(solution)/shard_map/jit(_pad)/pad | solution.py:321
  2.9 14.1 %rotate.1 = (f32[24,24,128]{2,1,0:T(8,128)}, f32[24,24,128]{2,1,0:T(8,128)}) custom-call(f32[108,128]{1,0:T(8,128)} %reshape.5.refs_0_, s32[24,640]{1,0:T(8,128)} %pad.4.refs_1_, f32[24,256]{1,0:T(8,128)} %constant.16.clone.refs_2_), custom_call_target="tpu_custom_call" | custom-call | tf_op jit(solution)/shard_map/rotate/pallas_call | solution.py:326
  17.0 26.2 %match.1 = f32[1,32,104]{2,1,0:T(8,128)} custom-call(f32[1,32,104]{2,1,0:T(8,128)} %refs_0_.1, f32[24,24,128]{2,1,0:T(8,128)} %get-tuple-element.7.refs_1_, f32[24,24,128]{2,1,0:T(8,128)} %get-tuple-element.8.refs_2_, f32[2,104,256]{2,1,0:T(8,128)} %constant.17.clone.refs_3_, f32[128,128]{1,0:T(8,128)} %constant.18.clone.refs_4_, ...), custom_call_target="tpu_custom_call" | custom-call | tf_op jit(solution)/shard_map/match/pallas_call | solution.py:346
  43.2 1.3 %copy.13 = f32[1,32,104]{2,1,0:T(8,128)} copy(f32[1,32,104]{2,1,0:T(8,128)} %match.1) | data formatting | bytes 26624
Async XLA Ops:
  0.0 1.8 %copy-start = (s32[1,13824]{1,0:T(1,128)S(1)}, s32[1,13824]{1,0:T(1,128)}, u32[]{:S(2)}) copy-start(s32[1,13824]{1,0:T(1,128)} %param.12) | copy-start | bytes 165892

commit v2 on v1

--- a/solution.py
+++ b/solution.py
@@ -94,55 +94,41 @@
     return jnp.dot(a, b, precision=highest, preferred_element_type=jnp.float32)
 
 
-def rotate_kernel(voxels, lead, table_ref, index_ref, dft_ref, straight_ref, crossed_ref, normed, rotated):
-    table = table_ref[...]
-    rows = table.shape[0]
-    flat = lax.broadcasted_iota(jnp.int32, table.shape, 0) * LANES + lax.broadcasted_iota(
-        jnp.int32, table.shape, 1
-    )
-    valid = flat < voxels
-    mean = jnp.sum(table, keepdims=True) / voxels
-    centred = jnp.where(valid, table - mean, 0.0)
+def split_table(template_ref, normed):
+    lines, edge = template_ref.shape
+    template = template_ref[...]
+    centred = template - jnp.sum(template, keepdims=True) / (lines * edge)
     normed[...] = centred / jnp.sqrt(jnp.sum(centred * centred, keepdims=True) + epsilon)
-    edge, width = index_ref.shape
-    tiles = [(s, c) for s in range(0, edge, 8) for c in range(0, width, LANES)]
-    lows, highs = [], []
-    for s, c in tiles:
-        index = index_ref[s : s + 8, c : c + LANES]
-        lows.append(index & (LANES - 1))
-        highs.append(index >> 7)
-
-    def step(h, held):
-        row = jnp.broadcast_to(normed[pl.ds(h, 1), :], (8, LANES))
-        return tuple(
-            jnp.where(high == h, jnp.take_along_axis(row, low, axis=1), value)
-            for low, high, value in zip(lows, highs, held)
-        )
-
-    zero = jnp.zeros((8, LANES), jnp.float32)
-    held = lax.fori_loop(0, rows, step, tuple(zero for _ in tiles))
-    for (s, c), value in zip(tiles, held):
-        rotated[s : s + 8, c : c + LANES] = value
-    spectrum = lax.dot_general(
-        rotated[...],
-        dft_ref[...],
-        (((0,), (0,)), ((), ())),
-        precision=highest,
+    table = jnp.concatenate([normed[pl.ds(j, lines // 8, stride=8), :] for j in range(8)], axis=1)
+    spare = round_up(lines // 8, 16) - lines // 8
+    table = jnp.concatenate([table, jnp.zeros((spare, 8 * edge), jnp.float32)], axis=0)
+    upper = table.astype(jnp.bfloat16)
+    lower = (table - upper.astype(jnp.float32)).astype(jnp.bfloat16)
+    return jnp.concatenate([upper, lower], axis=0)
+
+
+def look_up(pieces, index):
+    count, span = pieces.shape
+    width = index.shape[1]
+    high = ((index.astype(jnp.float32) + 0.5) * (1.0 / span)).astype(jnp.int32)
+    low = index - high * span
+    chosen = lax.broadcasted_iota(jnp.int32, (span, width), 0) == low
+    lanes = jnp.dot(
+        pieces,
+        jnp.where(chosen, 1.0, 0.0).astype(jnp.bfloat16),
         preferred_element_type=jnp.float32,
     )
-    size = spectrum.shape[1] // 2
-    if straight_ref.shape[0] > edge:
-        straight_ref[...] = jnp.zeros_like(straight_ref)
-        crossed_ref[...] = jnp.zeros_like(crossed_ref)
-    straight_ref[lead : lead + edge] = spectrum[: edge * edge, :size].reshape(edge, edge, size)
-    crossed_ref[lead : lead + edge] = spectrum[: edge * edge, size:].reshape(edge, edge, size)
+    lanes = lanes[: count // 2] + lanes[count // 2 :]
+    mine = lax.broadcasted_iota(jnp.int32, lanes.shape, 0) == high
+    return jnp.sum(jnp.where(mine, lanes, 0.0), axis=0, keepdims=True)
 
 
 def match_kernel(
     sizes,
     brick_ref,
-    straight_ref,
-    crossed_ref,
+    template_ref,
+    index_ref,
+    template_dft_ref,
     forward_ref,
     smoothing_ref,
     inverse_ref,
@@ -150,6 +136,11 @@
     score_dft_ref,
     box_ref,
     best_ref,
+    scaling_ref,
+    normed,
+    rotated,
+    straight_ref,
+    crossed_ref,
     pencils,
     tall,
     windows,
@@ -159,11 +150,12 @@
     totals,
     scores,
     arrived,
+    sems0,
     sems1,
     sems2,
     sems3,
 ):
-    orients, brows, bcols, edge, voxels, lead = sizes
+    orients, brows, bcols, edge, voxels, lead, taken = sizes
     half_edge = edge // 2
     rows, cols = brick_ref.shape[1:]
     tile_rows = windows.shape[1]
@@ -180,11 +172,22 @@
     def plane_peer(step):
         return {"orient": lax.rem(me + step, orients), "brow": row_id, "bcol": col_id}
 
+    windows[...] = jnp.zeros_like(windows)
     barrier = pltpu.get_barrier_semaphore()
     for step in range(1, group):
         pl.semaphore_signal(barrier, inc=1, device_id=brick_peer(step), device_id_type=MESH)
     for step in range(1, orients):
         pl.semaphore_signal(barrier, inc=1, device_id=plane_peer(step), device_id_type=MESH)
+
+    energy[...] = jnp.zeros_like(energy)
+    totals[...] = jnp.zeros_like(totals)
+    tall[...] = jnp.zeros_like(tall)
+    rotated[place] = jnp.zeros(rotated.shape[1:], jnp.float32)
+    share = index_ref.shape[1]
+    pieces = split_table(template_ref, normed)
+    for i in range(share):
+        rotated[place, i : i + 1, :] = look_up(pieces, index_ref[place, i : i + 1, :])
+
     pl.semaphore_wait(barrier, group + orients - 2)
 
     gathers = []
@@ -199,10 +202,19 @@
         )
         copy.start()
         gathers.append(copy)
+    shares = []
+    for step in range(1, group):
+        copy = pltpu.make_async_remote_copy(
+            src_ref=rotated.at[place],
+            dst_ref=rotated.at[place],
+            send_sem=sems0.at[0, step],
+            recv_sem=sems0.at[1, step],
+            device_id=brick_peer(step),
+            device_id_type=MESH,
+        )
+        copy.start()
+        shares.append(copy)
     pencils[col_id, row_id] = brick_ref[0]
-    energy[...] = jnp.zeros_like(energy)
-    totals[...] = jnp.zeros_like(totals)
-    tall[...] = jnp.zeros_like(tall)
     for copy in gathers:
         copy.wait_recv()
 
@@ -218,12 +230,14 @@
     ) + dot(imag * weights, inverse_ref[col_id, padded:, :])
     start = pl.multiple_of(row_id * rows, 8)
     windows[me] = tall[pl.ds(start, tile_rows), :]
+    idle = half_edge // 8 * 8 if brows == 2 else 0
+    filled = pl.ds(pl.multiple_of((brows - 1 - row_id) * idle, 8), tile_rows - idle)
 
     sends = []
     for step in range(1, orients):
         copy = pltpu.make_async_remote_copy(
-            src_ref=windows.at[me],
-            dst_ref=windows.at[me],
+            src_ref=windows.at[me, filled],
+            dst_ref=windows.at[me, filled],
             send_sem=sems2.at[0, step],
             recv_sem=sems2.at[1, step],
             device_id=plane_peer(step),
@@ -231,6 +245,25 @@
         )
         copy.start()
         sends.append(copy)
+
+    for copy in shares:
+        copy.wait_recv()
+    turned = None
+    for part in range(group):
+        term = lax.dot_general(
+            rotated[part],
+            template_dft_ref[part],
+            (((0,), (0,)), ((), ())),
+            precision=highest,
+            preferred_element_type=jnp.float32,
+        )
+        turned = term if turned is None else turned + term
+    size = turned.shape[1] // 2
+    if straight_ref.shape[0] > taken:
+        straight_ref[...] = jnp.zeros_like(straight_ref)
+        crossed_ref[...] = jnp.zeros_like(crossed_ref)
+    straight_ref[lead : lead + taken] = turned[:, :size].reshape(taken, edge, size)
+    crossed_ref[lead : lead + taken] = turned[:, size:].reshape(taken, edge, size)
 
     bunch = math.gcd(orients, 8)
 
@@ -250,7 +283,7 @@
                 near_part = spectrum[b : b + rows, :]
                 far_part = swapped[b : b + rows, :]
                 for z in range(bunch):
-                    a = plane - first - z + half_edge + lead
+                    a = plane - first - z + orients - 1
                     held[z] = held[z] + (
                         near_part * straight_ref[a, b : b + 1, :]
                         + far_part * crossed_ref[a, b : b + 1, :]
@@ -269,8 +302,8 @@
     def _(step):
         source = lax.rem(me - step + orients, orients)
         pltpu.make_async_remote_copy(
-            src_ref=windows.at[source],
-            dst_ref=windows.at[source],
+            src_ref=windows.at[source, filled],
+            dst_ref=windows.at[source, filled],
             send_sem=sems2.at[0, step],
             recv_sem=sems2.at[1, step],
             device_id=plane_peer(step),
@@ -278,7 +311,6 @@
         ).wait_recv()
         absorb(source)
 
-    size = spectrum.shape[1]
     scored = dot(totals[...].reshape(orients * rows, size), score_dft_ref[...])
     scores[...] = scored.reshape(orients, rows, cols)
     returns = []
@@ -301,8 +333,9 @@
     for step, copy in zip(range(1, orients), returns):
         copy.wait_recv()
         best = jnp.maximum(best, arrived[step])
-    best_ref[0] = best * scaling
-    for copy in gathers + sends + returns:
+    best_ref[0] = best
+    scaling_ref[0] = scaling
+    for copy in gathers + shares + sends + returns:
         copy.wait_send()
 
 
@@ -315,26 +348,20 @@
     length = cols * bcols
     size = cols + edge
     tile_rows = rows + edge
-    table_rows = round_up(voxels, LANES) // LANES
-    table = jnp.pad(template.reshape(-1), (0, table_rows * LANES - voxels)).reshape(table_rows, LANES)
-    width = round_up(edge * edge, LANES)
-    index = jnp.pad(voxel_maps[0].reshape(edge * edge, edge).T, ((0, 0), (0, width - edge * edge)))
-    lead = max(0, orients - 1 - half_edge)
-    trail = max(0, half_edge + orients - edge)
+    group = brows * bcols
+    share = -(-edge // group)
+    first = max(0, half_edge - orients + 1)
+    taken = min(edge, half_edge + orients) - first
+    lead = first - (half_edge - orients + 1)
+    index = voxel_maps.reshape(edge, edge, edge)[first : first + taken].reshape(taken * edge, edge).T
+    index = jnp.pad(index, ((0, share * group - edge), (0, 0))).reshape(group, share, taken * edge)
+    held = round_up(share, 8)
+    template_dft = np.zeros((group, held, 2 * size), np.float32)
+    for c, line in enumerate(template_table(edge, size)):
+        template_dft[c // share, c % share] = line
     vmem = pl.BlockSpec(memory_space=pltpu.VMEM)
-    spectra = jax.ShapeDtypeStruct((lead + edge + trail, edge, size), jnp.float32)
-    straight, crossed = pl.pallas_call(
-        lambda *refs: rotate_kernel(voxels, lead, *refs),
-        out_shape=(spectra, spectra),
-        in_specs=[vmem] * 3,
-        out_specs=(vmem, vmem),
-        scratch_shapes=[
-            pltpu.VMEM((table_rows, LANES), jnp.float32),
-            pltpu.VMEM((edge, width), jnp.float32),
-        ],
-        name="rotate",
-    )(table, index, jnp.asarray(template_table(edge, size)))
     constants = (
+        template_dft,
         forward_table(length, bcols),
         smoothing_table(length),
         windowed_inverse(length, bcols, half_edge),
@@ -342,13 +369,17 @@
         score_table(size, cols),
         box_table(size, cols, edge),
     )
-    sizes = (orients, brows, bcols, edge, voxels, lead)
-    return pl.pallas_call(
+    sizes = (orients, brows, bcols, edge, voxels, lead, taken)
+    best, scaling = pl.pallas_call(
         lambda *refs: match_kernel(sizes, *refs),
-        out_shape=jax.ShapeDtypeStruct((1, rows, cols), jnp.float32),
-        in_specs=[vmem] * 9,
-        out_specs=vmem,
+        out_shape=(jax.ShapeDtypeStruct((1, rows, cols), jnp.float32),) * 2,
+        in_specs=[vmem] * 10,
+        out_specs=(vmem, vmem),
         scratch_shapes=[
+            pltpu.VMEM((edge * edge, edge), jnp.float32),
+            pltpu.VMEM((group, held, taken * edge), jnp.float32),
+            pltpu.VMEM((2 * orients - 1, edge, size), jnp.float32),
+            pltpu.VMEM((2 * orients - 1, edge, size), jnp.float32),
             pltpu.VMEM((bcols, brows, rows, cols), jnp.float32),
             pltpu.VMEM((brows * rows + edge, size), jnp.float32),
             pltpu.VMEM((orients, tile_rows, size), jnp.float32),
@@ -358,13 +389,15 @@
             pltpu.VMEM((orients, rows, size), jnp.float32),
             pltpu.VMEM((orients, rows, cols), jnp.float32),
             pltpu.VMEM((orients, rows, cols), jnp.float32),
-            pltpu.SemaphoreType.DMA((2, brows * bcols)),
+            pltpu.SemaphoreType.DMA((2, group)),
+            pltpu.SemaphoreType.DMA((2, group)),
             pltpu.SemaphoreType.DMA((2, orients)),
             pltpu.SemaphoreType.DMA((2, orients)),
         ],
         compiler_params=pltpu.CompilerParams(collective_id=0, has_side_effects=True),
         name="match",
-    )(volume, straight, crossed, *(jnp.asarray(c) for c in constants))
+    )(volume, template.reshape(edge * edge, edge), index, *(jnp.asarray(c) for c in constants))
+    return best * scaling
 
 
 def solution(mesh):

time: 44.8 us -> 28.8 us (0.64)
  Pallas kernels: 40.3 us -> 25.4 us
  local copies, waits for them, and re-layouts: 4.05 us -> 1.79 us
  other arithmetic: 0.13 us -> 1.34 us
    pallas_call x2 -> x1, Pallas kernels: 40.3 us -> 25.4 us  [shards(): pl.pallas_call(lambda *refs: match_kernel(sizes, *refs), out_shape=(jax.S...]
    mul x0 -> x1, other arithmetic: none -> 1.34 us  [shards(): return best * scaling]
    unnamed x3 -> x0, local copies, waits for them, and re-layouts: 1.33 us -> none
    reshape x1 -> x2, local copies, waits for them, and re-layouts: 1.76 us -> 0.78 us  [the longest x1 0.65 us: shards(): jnp.pad(index, ((0, share * group - edge), (0, 0)))]
    slice x0 -> x1, local copies, waits for them, and re-layouts: none -> 0.91 us  [shards(): voxel_maps.reshape(edge, edge, edge)[first:first + taken]]
    pad x1 -> x0, local copies, waits for them, and re-layouts: 0.64 us -> none  [shards(): jnp.pad(voxel_maps[0].reshape(edge * edge, edge).T, ((0, 0), (0, width -...]
where the time goes in v2:
time: 28.8 us; the launch traced here: 28.6 us
  Pallas kernels  25.4 us (88%)
  local copies, waits for them, and re-layouts  1.79 us (6%)
  other arithmetic  1.34 us (5%)
    pallas_call x1, Pallas kernels, shards(): pl.pallas_call(lambda *refs: match_kernel(sizes, *refs), out_shape=(jax.S...  25.4 us
    mul x1, other arithmetic, shards(): return best * scaling  1.34 us
    slice x1, local copies, waits for them, and re-layouts, shards(): voxel_maps.reshape(edge, edge, edge)[first:first + taken]  0.91 us
    reshape x1, local copies, waits for them, and re-layouts, shards(): jnp.pad(index, ((0, share * group - edge), (0, 0)))  0.65 us

profile of v2, /device:TPU:0, one launch (start us, length us, event | category | flops | bytes accessed | tf_op | source)
XLA Modules:
  0.0 28.6 jit_solution(4206443245721589020)
XLA Ops:
  0.0 0.9 %slice_reduce_fusion = s32[8640]{0:T(1024)S(1)} fusion(s32[1,13824]{1,0:T(1,128)} %param.12), kind=kLoop, calls=%fused_computation | loop fusion | bytes 69120 | tf_op jit(solution)/shard_map/slice | solution.py:356
  0.9 0.1 reshape.13
  1.1 0.1 copy.12
  1.2 0.6 %reshape.14.refs_2_ = s32[4,6,360]{2,1,0:T(8,128)} reshape(s32[24,360]{1,0:T(8,128)S(1)} %copy.12) | data formatting | bytes 69120 | tf_op jit(solution)/shard_map/reshape | solution.py:357
  1.8 25.4 %match.1 = (f32[1,32,104]{2,1,0:T(8,128)}, f32[1,32,104]{2,1,0:T(8,128)}) custom-call(f32[1,32,104]{2,1,0:T(8,128)} %refs_0_.1, f32[576,24]{1,0:T(8,128)} %bitcast.3, s32[4,6,360]{2,1,0:T(8,128)} %reshape.14.refs_2_, f32[4,8,256]{2,1,0:T(8,128)} %constant.7.clone.refs_3_, f32[2,104,256]{2,1,0:T(8,128)} %constant.16.clone.refs_4_, ...), custom_call_target="tpu_custom_call" | custom-call | tf_op jit(solution)/shard_map/match/pallas_call | solution.py:373
  27.2 1.3 %mul.3 = f32[1,32,104]{2,1,0:T(8,128)} multiply(f32[1,32,104]{2,1,0:T(8,128)} %get-tuple-element.7, f32[1,32,104]{2,1,0:T(8,128)} %get-tuple-element.8) | non-fusion elementwise | flops 3328 | bytes 39936 | tf_op jit(solution)/shard_map/mul | solution.py:400

commit v3 on v2

--- a/solution.py
+++ b/solution.py
@@ -139,6 +139,7 @@
     scaling_ref,
     normed,
     rotated,
+    rotations,
     straight_ref,
     crossed_ref,
     pencils,
@@ -148,14 +149,11 @@
     swapped,
     energy,
     totals,
-    scores,
-    arrived,
     sems0,
     sems1,
     sems2,
-    sems3,
 ):
-    orients, brows, bcols, edge, voxels, lead, taken = sizes
+    orients, brows, bcols, edge, voxels, base, first, last = sizes
     half_edge = edge // 2
     rows, cols = brick_ref.shape[1:]
     tile_rows = windows.shape[1]
@@ -182,11 +180,9 @@
     energy[...] = jnp.zeros_like(energy)
     totals[...] = jnp.zeros_like(totals)
     tall[...] = jnp.zeros_like(tall)
-    rotated[place] = jnp.zeros(rotated.shape[1:], jnp.float32)
-    share = index_ref.shape[1]
+    if first > base or last < base + rotated.shape[0]:
+        rotated[...] = jnp.zeros_like(rotated)
     pieces = split_table(template_ref, normed)
-    for i in range(share):
-        rotated[place, i : i + 1, :] = look_up(pieces, index_ref[place, i : i + 1, :])
 
     pl.semaphore_wait(barrier, group + orients - 2)
 
@@ -202,19 +198,30 @@
         )
         copy.start()
         gathers.append(copy)
+    pencils[col_id, row_id] = brick_ref[0]
+    plane_voxels = edge * edge
+
+    @pl.loop(0, (last - first) // 2)
+    def _(pair):
+        start = pl.multiple_of((first + 2 * pair) * plane_voxels, 2 * plane_voxels)
+        found = look_up(pieces, index_ref[0:1, pl.ds(start, 2 * plane_voxels)])
+        for i in range(2):
+            rotated[first - base + 2 * pair + i] = found[:, i * plane_voxels : (i + 1) * plane_voxels]
+
     shares = []
-    for step in range(1, group):
+    for step in range(1, orients):
+        target = lax.rem(me + step, orients)
         copy = pltpu.make_async_remote_copy(
-            src_ref=rotated.at[place],
-            dst_ref=rotated.at[place],
+            src_ref=rotated.at[pl.ds(half_edge - target - base, orients)],
+            dst_ref=rotations.at[me],
             send_sem=sems0.at[0, step],
             recv_sem=sems0.at[1, step],
-            device_id=brick_peer(step),
+            device_id=plane_peer(step),
             device_id_type=MESH,
         )
         copy.start()
         shares.append(copy)
-    pencils[col_id, row_id] = brick_ref[0]
+    rotations[me] = rotated[pl.ds(half_edge - me - base, orients)]
     for copy in gathers:
         copy.wait_recv()
 
@@ -246,24 +253,30 @@
         copy.start()
         sends.append(copy)
 
-    for copy in shares:
-        copy.wait_recv()
-    turned = None
-    for part in range(group):
-        term = lax.dot_general(
-            rotated[part],
-            template_dft_ref[part],
-            (((0,), (0,)), ((), ())),
-            precision=highest,
-            preferred_element_type=jnp.float32,
+    def unfold(rotation):
+        planes = rotations[rotation][:, 0, :]
+        lines = jnp.concatenate(
+            [planes[:, b * edge : (b + 1) * edge] for b in range(edge)], axis=0
         )
-        turned = term if turned is None else turned + term
-    size = turned.shape[1] // 2
-    if straight_ref.shape[0] > taken:
-        straight_ref[...] = jnp.zeros_like(straight_ref)
-        crossed_ref[...] = jnp.zeros_like(crossed_ref)
-    straight_ref[lead : lead + taken] = turned[:, :size].reshape(taken, edge, size)
-    crossed_ref[lead : lead + taken] = turned[:, size:].reshape(taken, edge, size)
+        turned = dot(lines, template_dft_ref[...])
+        size = turned.shape[1] // 2
+        straight_ref[rotation] = turned[:, :size].reshape(edge, orients, size)
+        crossed_ref[rotation] = turned[:, size:].reshape(edge, orients, size)
+
+    unfold(me)
+
+    @pl.loop(1, orients)
+    def _(step):
+        source = lax.rem(me - step + orients, orients)
+        pltpu.make_async_remote_copy(
+            src_ref=rotated.at[pl.ds(half_edge - me - base, orients)],
+            dst_ref=rotations.at[source],
+            send_sem=sems0.at[0, step],
+            recv_sem=sems0.at[1, step],
+            device_id=plane_peer(step),
+            device_id_type=MESH,
+        ).wait_recv()
+        unfold(source)
 
     bunch = math.gcd(orients, 8)
 
@@ -277,19 +290,18 @@
         swapped[...] = pltpu.roll(transformed, transformed.shape[1] // 2, 1)
 
         def targets(piece):
-            first = piece * bunch
-            held = [totals[first + z] for z in range(bunch)]
+            lowest = piece * bunch
+            held = [totals[lowest + r] for r in range(bunch)]
             for b in range(edge):
                 near_part = spectrum[b : b + rows, :]
                 far_part = swapped[b : b + rows, :]
-                for z in range(bunch):
-                    a = plane - first - z + orients - 1
-                    held[z] = held[z] + (
-                        near_part * straight_ref[a, b : b + 1, :]
-                        + far_part * crossed_ref[a, b : b + 1, :]
+                for r in range(bunch):
+                    held[r] = held[r] + (
+                        near_part * straight_ref[lowest + r, b, pl.ds(plane, 1), :]
+                        + far_part * crossed_ref[lowest + r, b, pl.ds(plane, 1), :]
                     )
-            for z in range(bunch):
-                totals[first + z] = held[z]
+            for r in range(bunch):
+                totals[lowest + r] = held[r]
 
         if orients == bunch:
             targets(0)
@@ -311,31 +323,16 @@
         ).wait_recv()
         absorb(source)
 
-    scored = dot(totals[...].reshape(orients * rows, size), score_dft_ref[...])
-    scores[...] = scored.reshape(orients, rows, cols)
-    returns = []
-    for step in range(1, orients):
-        copy = pltpu.make_async_remote_copy(
-            src_ref=scores.at[lax.rem(me + step, orients)],
-            dst_ref=arrived.at[step],
-            send_sem=sems3.at[0, step],
-            recv_sem=sems3.at[1, step],
-            device_id=plane_peer(step),
-            device_id_type=MESH,
-        )
-        copy.start()
-        returns.append(copy)
     summed = energy[0:rows, :]
     for b in range(1, edge):
         summed = summed + energy[b : b + rows, :]
     scaling = lax.rsqrt(dot(summed, box_ref[...]) / voxels + epsilon)
-    best = scores[me]
-    for step, copy in zip(range(1, orients), returns):
-        copy.wait_recv()
-        best = jnp.maximum(best, arrived[step])
+    size = spectrum.shape[1]
+    scored = dot(totals[...].reshape(orients * rows, size), score_dft_ref[...])
+    best = jnp.max(scored.reshape(orients, rows, cols), axis=0)
     best_ref[0] = best
     scaling_ref[0] = scaling
-    for copy in gathers + shares + sends + returns:
+    for copy in gathers + shares + sends:
         copy.wait_send()
 
 
@@ -348,20 +345,14 @@
     length = cols * bcols
     size = cols + edge
     tile_rows = rows + edge
+    base = (half_edge - orients + 1) // 2 * 2
+    first = max(0, base)
+    last = min(edge, round_up(half_edge + orients, 2))
+    held = round_up(half_edge + orients, 2) - base
     group = brows * bcols
-    share = -(-edge // group)
-    first = max(0, half_edge - orients + 1)
-    taken = min(edge, half_edge + orients) - first
-    lead = first - (half_edge - orients + 1)
-    index = voxel_maps.reshape(edge, edge, edge)[first : first + taken].reshape(taken * edge, edge).T
-    index = jnp.pad(index, ((0, share * group - edge), (0, 0))).reshape(group, share, taken * edge)
-    held = round_up(share, 8)
-    template_dft = np.zeros((group, held, 2 * size), np.float32)
-    for c, line in enumerate(template_table(edge, size)):
-        template_dft[c // share, c % share] = line
     vmem = pl.BlockSpec(memory_space=pltpu.VMEM)
     constants = (
-        template_dft,
+        template_table(edge, size),
         forward_table(length, bcols),
         smoothing_table(length),
         windowed_inverse(length, bcols, half_edge),
@@ -369,7 +360,7 @@
         score_table(size, cols),
         box_table(size, cols, edge),
     )
-    sizes = (orients, brows, bcols, edge, voxels, lead, taken)
+    sizes = (orients, brows, bcols, edge, voxels, base, first, last)
     best, scaling = pl.pallas_call(
         lambda *refs: match_kernel(sizes, *refs),
         out_shape=(jax.ShapeDtypeStruct((1, rows, cols), jnp.float32),) * 2,
@@ -377,9 +368,10 @@
         out_specs=(vmem, vmem),
         scratch_shapes=[
             pltpu.VMEM((edge * edge, edge), jnp.float32),
-            pltpu.VMEM((group, held, taken * edge), jnp.float32),
-            pltpu.VMEM((2 * orients - 1, edge, size), jnp.float32),
-            pltpu.VMEM((2 * orients - 1, edge, size), jnp.float32),
+            pltpu.VMEM((held, 1, edge * edge), jnp.float32),
+            pltpu.VMEM((orients, orients, 1, edge * edge), jnp.float32),
+            pltpu.VMEM((orients, edge, orients, size), jnp.float32),
+            pltpu.VMEM((orients, edge, orients, size), jnp.float32),
             pltpu.VMEM((bcols, brows, rows, cols), jnp.float32),
             pltpu.VMEM((brows * rows + edge, size), jnp.float32),
             pltpu.VMEM((orients, tile_rows, size), jnp.float32),
@@ -387,16 +379,13 @@
             pltpu.VMEM((tile_rows, size), jnp.float32),
             pltpu.VMEM((tile_rows, size), jnp.float32),
             pltpu.VMEM((orients, rows, size), jnp.float32),
-            pltpu.VMEM((orients, rows, cols), jnp.float32),
-            pltpu.VMEM((orients, rows, cols), jnp.float32),
+            pltpu.SemaphoreType.DMA((2, orients)),
             pltpu.SemaphoreType.DMA((2, group)),
-            pltpu.SemaphoreType.DMA((2, group)),
-            pltpu.SemaphoreType.DMA((2, orients)),
             pltpu.SemaphoreType.DMA((2, orients)),
         ],
         compiler_params=pltpu.CompilerParams(collective_id=0, has_side_effects=True),
         name="match",
-    )(volume, template.reshape(edge * edge, edge), index, *(jnp.asarray(c) for c in constants))
+    )(volume, template.reshape(edge * edge, edge), voxel_maps, *(jnp.asarray(c) for c in constants))
     return best * scaling
 
 

time: 28.8 us -> 25.1 us (0.87)
  Pallas kernels: 25.4 us -> 23.5 us
  local copies, waits for them, and re-layouts: 1.79 us -> 0 us
    pallas_call x1, Pallas kernels: 25.4 us -> 23.5 us  [shards(): pl.pallas_call(lambda *refs: match_kernel(sizes, *refs), out_shape=(jax.S...]
    slice x1 -> x0, local copies, waits for them, and re-layouts: 0.91 us -> none  [shards(): voxel_maps.reshape(edge, edge, edge)[first:first + taken]]
    reshape x2 -> x0, local copies, waits for them, and re-layouts: 0.78 us -> none  [the longest x1 0.65 us: shards(): jnp.pad(index, ((0, share * group - edge), (0, 0)))]
where the time goes in v3:
time: 25.1 us; the launch traced here: 24.9 us
  Pallas kernels  23.5 us (94%)
  other arithmetic  1.34 us (5%)
    pallas_call x1, Pallas kernels, shards(): pl.pallas_call(lambda *refs: match_kernel(sizes, *refs), out_shape=(jax.S...  23.5 us
    mul x1, other arithmetic, shards(): return best * scaling  1.34 us

profile of v3, /device:TPU:0, one launch (start us, length us, event | category | flops | bytes accessed | tf_op | source)
XLA Modules:
  0.0 24.9 jit_solution(6386257882405536129)
XLA Ops:
  0.0 23.5 %match.1 = (f32[1,32,104]{2,1,0:T(8,128)}, f32[1,32,104]{2,1,0:T(8,128)}) custom-call(f32[1,32,104]{2,1,0:T(8,128)} %refs_0_.1, f32[576,24]{1,0:T(8,128)} %bitcast.1, s32[1,13824]{1,0:T(1,128)} %refs_2_.1, f32[24,256]{1,0:T(8,128)} %constant.14.clone.refs_3_, f32[2,104,256]{2,1,0:T(8,128)} %constant.15.clone.refs_4_, f32[128,128]{1,0:T(8,128)} %constant.16.clone.refs_5_, ...), custom_call_target="tpu_custom_call" | custom-call | tf_op jit(solution)/shard_map/match/pallas_call | solution.py:364
  23.5 1.3 %mul.3 = f32[1,32,104]{2,1,0:T(8,128)} multiply(f32[1,32,104]{2,1,0:T(8,128)} %get-tuple-element.7, f32[1,32,104]{2,1,0:T(8,128)} %get-tuple-element.8) | non-fusion elementwise | flops 3328 | bytes 39936 | tf_op jit(solution)/shard_map/mul | solution.py:389

commit v4 on v3

--- a/solution.py
+++ b/solution.py
@@ -184,6 +184,16 @@
         rotated[...] = jnp.zeros_like(rotated)
     pieces = split_table(template_ref, normed)
 
+    plane_voxels = edge * edge
+
+    @pl.loop(0, (last - first) // 2)
+    def _(pair):
+        start = pl.multiple_of((first + 2 * pair) * plane_voxels, 2 * plane_voxels)
+        found = look_up(pieces, index_ref[0:1, pl.ds(start, 2 * plane_voxels)])
+        for i in range(2):
+            rotated[first - base + 2 * pair + i] = found[:, i * plane_voxels : (i + 1) * plane_voxels]
+
+    rotations[me] = rotated[pl.ds(half_edge - me - base, orients)]
     pl.semaphore_wait(barrier, group + orients - 2)
 
     gathers = []
@@ -199,29 +209,21 @@
         copy.start()
         gathers.append(copy)
     pencils[col_id, row_id] = brick_ref[0]
-    plane_voxels = edge * edge
-
-    @pl.loop(0, (last - first) // 2)
-    def _(pair):
-        start = pl.multiple_of((first + 2 * pair) * plane_voxels, 2 * plane_voxels)
-        found = look_up(pieces, index_ref[0:1, pl.ds(start, 2 * plane_voxels)])
-        for i in range(2):
-            rotated[first - base + 2 * pair + i] = found[:, i * plane_voxels : (i + 1) * plane_voxels]
-
+    parts = brows if orients % brows == 0 else 1
+    part_planes = orients // parts
     shares = []
     for step in range(1, orients):
         target = lax.rem(me + step, orients)
         copy = pltpu.make_async_remote_copy(
-            src_ref=rotated.at[pl.ds(half_edge - target - base, orients)],
-            dst_ref=rotations.at[me],
-            send_sem=sems0.at[0, step],
-            recv_sem=sems0.at[1, step],
+            src_ref=rotated.at[pl.ds(half_edge - target - base + lax.rem(row_id, parts) * part_planes, part_planes)],
+            dst_ref=rotations.at[me, pl.ds(lax.rem(row_id, parts) * part_planes, part_planes)],
+            send_sem=sems0.at[0, 0, step],
+            recv_sem=sems0.at[0, 1, step],
             device_id=plane_peer(step),
             device_id_type=MESH,
         )
         copy.start()
         shares.append(copy)
-    rotations[me] = rotated[pl.ds(half_edge - me - base, orients)]
     for copy in gathers:
         copy.wait_recv()
 
@@ -265,18 +267,33 @@
 
     unfold(me)
 
+    def share_of(step, turn):
+        source = lax.rem(me - step + orients, orients)
+        owner = lax.rem(row_id, parts) * part_planes
+        block = rotations.at[source, pl.ds(owner, part_planes)]
+        to = plane_peer(step)
+        if turn:
+            to = {"orient": me, "brow": lax.rem(row_id + turn, brows), "bcol": col_id}
+        return pltpu.make_async_remote_copy(
+            src_ref=block,
+            dst_ref=block,
+            send_sem=sems0.at[turn, 0, step],
+            recv_sem=sems0.at[turn, 1, step],
+            device_id=to,
+            device_id_type=MESH,
+        )
+
     @pl.loop(1, orients)
     def _(step):
-        source = lax.rem(me - step + orients, orients)
-        pltpu.make_async_remote_copy(
-            src_ref=rotated.at[pl.ds(half_edge - me - base, orients)],
-            dst_ref=rotations.at[source],
-            send_sem=sems0.at[0, step],
-            recv_sem=sems0.at[1, step],
-            device_id=plane_peer(step),
-            device_id_type=MESH,
-        ).wait_recv()
-        unfold(source)
+        share_of(step, 0).wait_recv()
+        for turn in range(1, parts):
+            share_of(step, turn).start()
+
+    @pl.loop(1, orients)
+    def _(step):
+        for turn in range(1, parts):
+            share_of(step, turn).wait()
+        unfold(lax.rem(me - step + orients, orients))
 
     bunch = math.gcd(orients, 8)
 
@@ -379,7 +396,7 @@
             pltpu.VMEM((tile_rows, size), jnp.float32),
             pltpu.VMEM((tile_rows, size), jnp.float32),
             pltpu.VMEM((orients, rows, size), jnp.float32),
-            pltpu.SemaphoreType.DMA((2, orients)),
+            pltpu.SemaphoreType.DMA((brows, 2, orients)),
             pltpu.SemaphoreType.DMA((2, group)),
             pltpu.SemaphoreType.DMA((2, orients)),
         ],

time: 25.1 us -> 25.5 us (1.016)
  Pallas kernels: 23.5 us -> 23.9 us
    pallas_call x1, Pallas kernels: 23.5 us -> 23.9 us  [shards(): pl.pallas_call(lambda *refs: match_kernel(sizes, *refs), out_shape=(jax.S...]
where the time goes in v4:
time: 25.5 us; the launch traced here: 25.2 us
  Pallas kernels  23.9 us (94%)
  other arithmetic  1.34 us (5%)
    pallas_call x1, Pallas kernels, shards(): pl.pallas_call(lambda *refs: match_kernel(sizes, *refs), out_shape=(jax.S...  23.9 us
    mul x1, other arithmetic, shards(): return best * scaling  1.34 us

profile of v4, /device:TPU:0, one launch (start us, length us, event | category | flops | bytes accessed | tf_op | source)
XLA Modules:
  0.0 25.2 jit_solution(11557788736167221079)
XLA Ops:
  0.0 23.9 %match.1 = (f32[1,32,104]{2,1,0:T(8,128)}, f32[1,32,104]{2,1,0:T(8,128)}) custom-call(f32[1,32,104]{2,1,0:T(8,128)} %refs_0_.1, f32[576,24]{1,0:T(8,128)} %bitcast.1, s32[1,13824]{1,0:T(1,128)} %refs_2_.1, f32[24,256]{1,0:T(8,128)} %constant.14.clone.refs_3_, f32[2,104,256]{2,1,0:T(8,128)} %constant.15.clone.refs_4_, f32[128,128]{1,0:T(8,128)} %constant.16.clone.refs_5_, ...), custom_call_target="tpu_custom_call" | custom-call | tf_op jit(solution)/shard_map/match/pallas_call | solution.py:381
  23.9 1.3 %mul.3 = f32[1,32,104]{2,1,0:T(8,128)} multiply(f32[1,32,104]{2,1,0:T(8,128)} %get-tuple-element.7, f32[1,32,104]{2,1,0:T(8,128)} %get-tuple-element.8) | non-fusion elementwise | flops 3328 | bytes 39936 | tf_op jit(solution)/shard_map/mul | solution.py:406

commit v5 on v4

--- a/solution.py
+++ b/solution.py
@@ -125,6 +125,7 @@
 
 def match_kernel(
     sizes,
+    fetch,
     brick_ref,
     template_ref,
     index_ref,
@@ -167,8 +168,16 @@
         other = lax.rem(place + step, group)
         return {"orient": me, "brow": other // bcols, "bcol": lax.rem(other, bcols)}
 
+    def partner(step):
+        assert orients & (orients - 1) == 0
+        other, weight = 0, 1
+        while weight < orients:
+            other = other + lax.rem(me // weight + step // weight, 2) * weight
+            weight *= 2
+        return other
+
     def plane_peer(step):
-        return {"orient": lax.rem(me + step, orients), "brow": row_id, "bcol": col_id}
+        return {"orient": partner(step), "brow": row_id, "bcol": col_id}
 
     windows[...] = jnp.zeros_like(windows)
     barrier = pltpu.get_barrier_semaphore()
@@ -177,6 +186,7 @@
     for step in range(1, orients):
         pl.semaphore_signal(barrier, inc=1, device_id=plane_peer(step), device_id_type=MESH)
 
+    fetch()
     energy[...] = jnp.zeros_like(energy)
     totals[...] = jnp.zeros_like(totals)
     tall[...] = jnp.zeros_like(tall)
@@ -184,16 +194,6 @@
         rotated[...] = jnp.zeros_like(rotated)
     pieces = split_table(template_ref, normed)
 
-    plane_voxels = edge * edge
-
-    @pl.loop(0, (last - first) // 2)
-    def _(pair):
-        start = pl.multiple_of((first + 2 * pair) * plane_voxels, 2 * plane_voxels)
-        found = look_up(pieces, index_ref[0:1, pl.ds(start, 2 * plane_voxels)])
-        for i in range(2):
-            rotated[first - base + 2 * pair + i] = found[:, i * plane_voxels : (i + 1) * plane_voxels]
-
-    rotations[me] = rotated[pl.ds(half_edge - me - base, orients)]
     pl.semaphore_wait(barrier, group + orients - 2)
 
     gathers = []
@@ -209,11 +209,21 @@
         copy.start()
         gathers.append(copy)
     pencils[col_id, row_id] = brick_ref[0]
+    plane_voxels = edge * edge
+
+    @pl.loop(0, (last - first) // 2)
+    def _(pair):
+        start = pl.multiple_of((first + 2 * pair) * plane_voxels, 2 * plane_voxels)
+        found = look_up(pieces, index_ref[0:1, pl.ds(start, 2 * plane_voxels)])
+        for i in range(2):
+            rotated[first - base + 2 * pair + i] = found[:, i * plane_voxels : (i + 1) * plane_voxels]
+
+    rotations[me] = rotated[pl.ds(half_edge - me - base, orients)]
     parts = brows if orients % brows == 0 else 1
     part_planes = orients // parts
     shares = []
     for step in range(1, orients):
-        target = lax.rem(me + step, orients)
+        target = partner(step)
         copy = pltpu.make_async_remote_copy(
             src_ref=rotated.at[pl.ds(half_edge - target - base + lax.rem(row_id, parts) * part_planes, part_planes)],
             dst_ref=rotations.at[me, pl.ds(lax.rem(row_id, parts) * part_planes, part_planes)],
@@ -268,7 +278,7 @@
     unfold(me)
 
     def share_of(step, turn):
-        source = lax.rem(me - step + orients, orients)
+        source = partner(step)
         owner = lax.rem(row_id, parts) * part_planes
         block = rotations.at[source, pl.ds(owner, part_planes)]
         to = plane_peer(step)
@@ -293,7 +303,7 @@
     def _(step):
         for turn in range(1, parts):
             share_of(step, turn).wait()
-        unfold(lax.rem(me - step + orients, orients))
+        unfold(partner(step))
 
     bunch = math.gcd(orients, 8)
 
@@ -329,7 +339,7 @@
 
     @pl.loop(1, orients)
     def _(step):
-        source = lax.rem(me - step + orients, orients)
+        source = partner(step)
         pltpu.make_async_remote_copy(
             src_ref=windows.at[source, filled],
             dst_ref=windows.at[source, filled],
@@ -351,6 +361,23 @@
     scaling_ref[0] = scaling
     for copy in gathers + shares + sends:
         copy.wait_send()
+
+
+def staged(sizes, count, *refs):
+    sources, results = refs[:count], refs[count : count + 2]
+    held, rest = refs[count + 2 : 2 * count + 2], refs[2 * count + 2 : -1]
+    copies = [
+        pltpu.make_async_copy(source, target, refs[-1].at[i])
+        for i, (source, target) in enumerate(zip(sources, held))
+    ]
+    for copy in copies:
+        copy.start()
+
+    def fetch():
+        for copy in copies:
+            copy.wait()
+
+    match_kernel(sizes, fetch, *held, *results, *rest)
 
 
 def shards(volume, template, voxel_maps):
@@ -378,12 +405,15 @@
         box_table(size, cols, edge),
     )
     sizes = (orients, brows, bcols, edge, voxels, base, first, last)
+    operands = (volume, template.reshape(edge * edge, edge), voxel_maps)
+    operands += tuple(jnp.asarray(c) for c in constants)
     best, scaling = pl.pallas_call(
-        lambda *refs: match_kernel(sizes, *refs),
+        lambda *refs: staged(sizes, len(operands), *refs),
         out_shape=(jax.ShapeDtypeStruct((1, rows, cols), jnp.float32),) * 2,
-        in_specs=[vmem] * 10,
+        in_specs=[pl.BlockSpec(memory_space=pl.ANY)] * len(operands),
         out_specs=(vmem, vmem),
-        scratch_shapes=[
+        scratch_shapes=[pltpu.VMEM(x.shape, x.dtype) for x in operands]
+        + [
             pltpu.VMEM((edge * edge, edge), jnp.float32),
             pltpu.VMEM((held, 1, edge * edge), jnp.float32),
             pltpu.VMEM((orients, orients, 1, edge * edge), jnp.float32),
@@ -399,10 +429,11 @@
             pltpu.SemaphoreType.DMA((brows, 2, orients)),
             pltpu.SemaphoreType.DMA((2, group)),
             pltpu.SemaphoreType.DMA((2, orients)),
+            pltpu.SemaphoreType.DMA((len(operands),)),
         ],
         compiler_params=pltpu.CompilerParams(collective_id=0, has_side_effects=True),
         name="match",
-    )(volume, template.reshape(edge * edge, edge), voxel_maps, *(jnp.asarray(c) for c in constants))
+    )(*operands)
     return best * scaling
 
 

time: 25.5 us -> 25 us (0.980)
  Pallas kernels: 23.9 us -> 23.3 us
    pallas_call x1, Pallas kernels: 23.9 us -> 23.3 us  [shards(): pl.pallas_call(lambda *refs: staged(sizes, len(operands), *refs), out_sha...]
where the time goes in v5:
time: 25 us; the launch traced here: 24.7 us
  Pallas kernels  23.3 us (93%)
  other arithmetic  1.34 us (5%)
    pallas_call x1, Pallas kernels, shards(): pl.pallas_call(lambda *refs: staged(sizes, len(operands), *refs), out_sha...  23.3 us
    mul x1, other arithmetic, shards(): return best * scaling  1.34 us

profile of v5, /device:TPU:0, one launch (start us, length us, event | category | flops | bytes accessed | tf_op | source)
XLA Modules:
  0.0 24.7 jit_solution(1144006879459632551)
XLA Ops:
  0.0 23.3 %match.1 = (f32[1,32,104]{2,1,0:T(8,128)}, f32[1,32,104]{2,1,0:T(8,128)}) custom-call(f32[1,32,104]{2,1,0:T(8,128)} %refs_0_.1, f32[576,24]{1,0:T(8,128)} %bitcast.1, s32[1,13824]{1,0:T(1,128)} %refs_2_.1, f32[24,256]{1,0:T(8,128)} %constant.14.clone.refs_3_, f32[2,104,256]{2,1,0:T(8,128)} %constant.15.clone.refs_4_, f32[128,128]{1,0:T(8,128)} %constant.16.clone.refs_5_, ...), custom_call_target="tpu_custom_call" | custom-call | tf_op jit(solution)/shard_map/match/pallas_call | solution.py:410
  23.3 1.3 %mul.3 = f32[1,32,104]{2,1,0:T(8,128)} multiply(f32[1,32,104]{2,1,0:T(8,128)} %get-tuple-element.7, f32[1,32,104]{2,1,0:T(8,128)} %get-tuple-element.8) | non-fusion elementwise | flops 3328 | bytes 39936 | tf_op jit(solution)/shard_map/mul | solution.py:437

commit v6 on v5

--- a/solution.py
+++ b/solution.py
@@ -270,7 +270,7 @@
         lines = jnp.concatenate(
             [planes[:, b * edge : (b + 1) * edge] for b in range(edge)], axis=0
         )
-        turned = dot(lines, template_dft_ref[...])
+        turned = dot_short(lines, template_dft_ref[...])
         size = turned.shape[1] // 2
         straight_ref[rotation] = turned[:, :size].reshape(edge, orients, size)
         crossed_ref[rotation] = turned[:, size:].reshape(edge, orients, size)
@@ -312,7 +312,7 @@
         gap = plane - me
         near = jnp.logical_and(gap >= -half_edge, gap < half_edge).astype(jnp.float32)
         energy[...] += window * window * near
-        transformed = dot(window, volume_dft_ref[...])
+        transformed = dot_short(window, volume_dft_ref[...])
         spectrum[...] = transformed
         swapped[...] = pltpu.roll(transformed, transformed.shape[1] // 2, 1)
 
@@ -355,12 +355,16 @@
         summed = summed + energy[b : b + rows, :]
     scaling = lax.rsqrt(dot(summed, box_ref[...]) / voxels + epsilon)
     size = spectrum.shape[1]
-    scored = dot(totals[...].reshape(orients * rows, size), score_dft_ref[...])
+    scored = dot_short(totals[...].reshape(orients * rows, size), score_dft_ref[...])
     best = jnp.max(scored.reshape(orients, rows, cols), axis=0)
     best_ref[0] = best
     scaling_ref[0] = scaling
     for copy in gathers + shares + sends:
         copy.wait_send()
+
+
+def dot_short(a, b):
+    return jnp.dot(a, b, precision=lax.Precision.HIGH, preferred_element_type=jnp.float32)
 
 
 def staged(sizes, count, *refs):

time: 25 us -> 24.1 us (0.964)
  Pallas kernels: 23.3 us -> 22.4 us
    pallas_call x1, Pallas kernels: 23.3 us -> 22.4 us  [shards(): pl.pallas_call(lambda *refs: staged(sizes, len(operands), *refs), out_sha...]
where the time goes in v6:
time: 24.1 us; the launch traced here: 23.7 us
  Pallas kernels  22.4 us (93%)
  other arithmetic  1.34 us (6%)
    pallas_call x1, Pallas kernels, shards(): pl.pallas_call(lambda *refs: staged(sizes, len(operands), *refs), out_sha...  22.4 us
    mul x1, other arithmetic, shards(): return best * scaling  1.34 us

profile of v6, /device:TPU:0, one launch (start us, length us, event | category | flops | bytes accessed | tf_op | source)
XLA Modules:
  0.0 23.7 jit_solution(17670498551316499539)
XLA Ops:
  0.0 22.4 %match.1 = (f32[1,32,104]{2,1,0:T(8,128)}, f32[1,32,104]{2,1,0:T(8,128)}) custom-call(f32[1,32,104]{2,1,0:T(8,128)} %refs_0_.1, f32[576,24]{1,0:T(8,128)} %bitcast.1, s32[1,13824]{1,0:T(1,128)} %refs_2_.1, f32[24,256]{1,0:T(8,128)} %constant.14.clone.refs_3_, f32[2,104,256]{2,1,0:T(8,128)} %constant.15.clone.refs_4_, f32[128,128]{1,0:T(8,128)} %constant.16.clone.refs_5_, ...), custom_call_target="tpu_custom_call" | custom-call | tf_op jit(solution)/shard_map/match/pallas_call | solution.py:414
  22.4 1.3 %mul.3 = f32[1,32,104]{2,1,0:T(8,128)} multiply(f32[1,32,104]{2,1,0:T(8,128)} %get-tuple-element.7, f32[1,32,104]{2,1,0:T(8,128)} %get-tuple-element.8) | non-fusion elementwise | flops 3328 | bytes 39936 | tf_op jit(solution)/shard_map/mul | solution.py:441
